TPU v7x, 32 devices: a whole 2x2x4 slice. The times are simulated.
32 devices in a mesh: parts: 2 (over y), wide: 4 (over z), narrow: 2 (over x), pair: 2 (over core).
Axes of the slice: x: 2, y: 2, z: 4, core: 2. Of those that a mesh axis runs over, the one named last changes fastest.
Arguments:
- low_sino: bfloat16 [8, 24, 32, 512], P(('parts', 'wide'), None, None, ('narrow', 'pair')), parts along dimension 0, may hold values from -6 to 6
- angle_weight: bfloat16 [4, 24, 24], replicated, may hold values from -1.25 to 1.25
- angle_bias: float32 [24], replicated, may hold values from -3 to 3
- column_weight: bfloat16 [4, 24, 24], replicated, may hold values from -0.875 to 0.875
- column_bias: float32 [24], replicated, may hold values from -3 to 3
- head_weight: float32 [24], replicated, may hold values from -1.25 to 1.25
- sparse_views: int32 [4, 16], P(('parts', 'narrow')), parts along dimension 0, may hold values from 0 to 7
- measured: float32 [32, 16, 512], P('parts', 'wide', ('narrow', 'pair')), parts along dimension 0, may hold values from -6 to 6
- row_weights: float32 [512, 512], P(('narrow', 'pair')), may hold values from -0.25 to 0.25
Outputs:
- predicted: float32 [16, 16, 512], P('parts', 'wide', ('narrow', 'pair')), parts along dimension 0
- adjoint: float32 [32, 16, 512], P('parts', 'wide', ('narrow', 'pair')), parts along dimension 0
There are 2 independent parts, one for each index of `parts`. A program takes and returns all parts, laid end to end along the dimension named above; an argument that names none is the same for every part. Nothing has to cross between parts.
All inputs are finite; a program needn't handle non-finite values.
Results may differ from a plain program's by a relative error of at most 0.0034.
Values may be sent and summed in bfloat16 or wider, within the bound.
A program may use at most 64 MiB of HBM per device.

v0:
```python
import jax
import jax.numpy as jnp
from jax import lax
from jax.sharding import PartitionSpec as P


def from_behind(block, axis, distance):
    devices = range(lax.axis_size(axis))
    route = [((i - distance) % len(devices), i) for i in devices]
    return lax.ppermute(block, axis, route)


def leaky_relu(values):
    return jnp.where(values > 0, values, 0.1 * values)


def channel_mix(inputs, weight):
    return jnp.einsum("vcwr,cd->vdwr", inputs, weight, preferred_element_type=jnp.float32)


def upsample(current, previous, weight, bias_values):
    even_views = channel_mix(current, weight[0]) + channel_mix(previous, weight[2])
    odd_views = channel_mix(current, weight[1]) + channel_mix(previous, weight[3])
    stacked = jnp.stack([even_views, odd_views], axis=1) + bias_values[None, None, :, None, None]
    return (
        leaky_relu(stacked)
        .reshape(2 * current.shape[0], current.shape[1], current.shape[2], current.shape[3])
        .astype(jnp.bfloat16)
    )


def detector_head(padded, col_count, column_weight, column_bias, head_weight):
    summed = channel_mix(padded[:, :, 0:col_count:2], column_weight[0])
    for tap_index in range(1, 4):
        summed = summed + channel_mix(
            padded[:, :, tap_index : tap_index + col_count : 2], column_weight[tap_index]
        )
    hidden = leaky_relu(summed + column_bias[None, :, None, None])
    return jnp.sum(hidden * head_weight[None, :, None, None], axis=1)


def local(
    low_sino,
    angle_weight,
    angle_bias,
    column_weight,
    column_bias,
    head_weight,
    sparse_views,
    measured,
    row_weights,
):
    last_view = from_behind(low_sino, "wide", 1)
    previous = jnp.concatenate([last_view, low_sino[:-1]], axis=0)
    upsampled = upsample(low_sino, previous, angle_weight, angle_bias)
    padded = jnp.pad(upsampled, ((0, 0), (0, 0), (1, 1), (0, 0)))
    own_views = detector_head(padded, upsampled.shape[2], column_weight, column_bias, head_weight)
    predicted = lax.all_to_all(own_views, "wide", split_axis=1, concat_axis=0, tiled=True)
    residual_slab = jnp.take(predicted, sparse_views[0], axis=0) - measured
    adjoint = jnp.einsum(
        "kjr,zr->kjz",
        lax.all_gather(residual_slab, ("narrow", "pair"), axis=2, tiled=True),
        row_weights,
        precision=lax.Precision.HIGHEST,
    )
    return (predicted, adjoint)


def solution(mesh):
    in_specs = (
        P(("parts", "wide"), None, None, ("narrow", "pair")),
        P(),
        P(),
        P(),
        P(),
        P(),
        P(("parts", "narrow"), None),
        P("parts", "wide", ("narrow", "pair")),
        P(("narrow", "pair"), None),
    )
    out_specs = (P("parts", "wide", ("narrow", "pair")), P("parts", "wide", ("narrow", "pair")))
    return jax.shard_map(local, mesh=mesh, in_specs=in_specs, out_specs=out_specs, check_vma=False)
```

profile of v0, /device:TPU:0, one launch (start us, length us, event | category | flops | bytes accessed | tf_op | source)
XLA Modules:
  0.0 31.7 jit_solution(15347137212192712056)
XLA Ops:
  0.6 0.0 copy-start
  0.6 0.0 copy-start.1
  0.7 0.0 copy-start.4
  0.7 1.1 %copy.58 = bf16[1,24,32,128]{3,1,2,0:T(8,128)(2,1)S(1)} copy(bf16[1,24,32,128]{3,2,1,0:T(8,128)(2,1)} %param.9) | data formatting | bytes 393216 | tf_op args[0]
  1.7 3.1 %collective-permute-start = (bf16[1,24,32,128]{3,1,2,0:T(8,128)(2,1)S(1)}, bf16[1,24,32,128]{3,1,2,0:T(8,128)(2,1)S(1)}, u32[]{:S(2)}, u32[]{:S(2)}) collective-permute-start(bf16[1,24,32,128]{3,1,2,0:T(8,128)(2,1)S(1)} %copy.58), channel_id=1, source_target_pairs={{12,0},{0,4},{4,8},{8,12},{13,1},{1,5},{5,9},{9,13},{14,2},{2,6},{... | collective-permute-start | bytes 589832 | tf_op jit(solution)/shard_map/ppermute | solution.py:10
  4.8 0.0 copy-done.1
  4.8 0.0 copy-done.4
  4.8 0.2 fusion.12
  5.1 0.0 copy-start.7
  5.1 0.2 fusion.14
  5.3 0.4 %copy-done.7 = s32[1,16]{1,0:T(1,128)S(1)} copy-done((s32[1,16]{1,0:T(1,128)S(1)}, s32[1,16]{1,0:T(1,128)}, u32[]{:S(2)}) %copy-start.7) | copy-done | bytes 88
  5.8 6.0 %collective-permute-done = bf16[1,24,32,128]{3,1,2,0:T(8,128)(2,1)S(1)} collective-permute-done((bf16[1,24,32,128]{3,1,2,0:T(8,128)(2,1)S(1)}, bf16[1,24,32,128]{3,1,2,0:T(8,128)(2,1)S(1)}, u32[]{:S(2)}, u32[]{:S(2)}) %collective-permute-start) | collective-permute-done | bytes 196640 | tf_op jit(solution)/shard_map/ppermute | solution.py:10
  11.8 0.2 fusion
  12.0 0.0 copy-start.6
  12.0 0.2 fusion.1
  12.3 0.4 %copy-done.6 = f32[24]{0:T(128)S(1)} copy-done((f32[24]{0:T(128)S(1)}, f32[24]{0:T(128)}, u32[]{:S(2)}) %copy-start.6) | copy-done | bytes 120
  12.7 0.0 copy-start.5
  12.7 0.2 fusion.4
  12.9 0.5 %copy-done.5 = bf16[4,24,24]{2,1,0:T(8,128)(2,1)S(1)} copy-done((bf16[4,24,24]{2,1,0:T(8,128)(2,1)S(1)}, bf16[4,24,24]{2,1,0:T(8,128)(2,1)}, u32[]{:S(2)}) %copy-start.5) | copy-done | bytes 4632
  13.4 0.2 fusion.9
  13.7 0.2 convolution_add_fusion.2
  13.9 0.0 copy-start.8
  13.9 0.0 copy-start.9
  13.9 0.3 convolution_add_fusion.1
  14.2 0.4 %copy-done.8 = f32[24]{0:T(128)S(1)} copy-done((f32[24]{0:T(128)S(1)}, f32[24]{0:T(128)}, u32[]{:S(2)}) %copy-start.8) | copy-done | bytes 120
  14.6 0.0 copy-done.9
  14.6 0.3 %fusion.6 = f32[2,16,128]{2,1,0:T(8,128)S(1)} fusion(f32[2,16,128,24]{2,3,1,0:T(8,128)S(1)} %convolution_add_fusion.1, bf16[2,24,32,128]{3,1,2,0:T(8,128)(2,1)S(1)} %fusion.4, f32[24]{0:T(128)S(1)} %copy-done.8, f32[24]{0:T(128)S(1)} %copy-done.9, bf16[4,24,24]{2,1,0:T(8,128)(2,1)S(1)} %copy-done.5), kind=kOutput, calls=%fused_computation.15 | convolution fusion | flops 5402624 | bytes 809984 | tf_op jit(solution)/shard_map/vcwr,cd->vdwr/dot_general | solution.py:18
  14.9 0.6 %copy.66 = f32[2,16,128]{2,0,1:T(2,128)} copy(f32[2,16,128]{2,1,0:T(8,128)S(1)} %fusion.6) | data formatting | bytes 32768 | tf_op jit(solution)/shard_map/reduce_sum | solution.py:39
  15.5 3.3 %all-to-all-start = ((f32[2,16,128]{2,0,1:T(2,128)}), f32[2,16,128]{2,0,1:T(2,128)S(1)}, u32[]{:S(2)}, u32[]{:S(2)}) async-start(f32[2,16,128]{2,0,1:T(2,128)} %copy.66), calls=%async_computation | async-start | bytes 32768 | tf_op jit(solution)/shard_map/all_to_all | solution.py:58
  18.8 5.6 %all-to-all-done = f32[2,16,128]{2,0,1:T(2,128)S(1)} async-done(((f32[2,16,128]{2,0,1:T(2,128)}), f32[2,16,128]{2,0,1:T(2,128)S(1)}, u32[]{:S(2)}, u32[]{:S(2)}) %all-to-all-start) | async-done | bytes 16416 | tf_op jit(solution)/shard_map/all_to_all | solution.py:58
  24.4 0.0 copy-start.2
  24.4 0.0 copy-start.3
  24.4 0.6 %gather_fusion = f32[16,4,128]{2,1,0:T(4,128)S(1)} fusion(f32[8,4,128]{2,1,0:T(4,128)S(1)} %bitcast.86, s32[1024]{0:T(1024)S(1)} %pad_clamp_fusion), kind=kCustom, calls=%fused_computation | custom fusion | bytes 65600 | tf_op jit(solution)/shard_map/jit(_take)/gather | solution.py:59
  25.0 0.0 copy-done.2
  25.0 0.2 copy-done.3
  25.1 0.1 copy_subtract_fusion
  25.2 5.4 %all_gather.3 = f32[16,4,512]{2,0,1:T(8,128)S(1)} all-gather(f32[16,4,128]{2,0,1:T(8,128)S(1)} %copy_subtract_fusion), channel_id=1, replica_groups=mesh['parts'=2,'wide'=4,'narrow'=2,'pair'=2] {'narrow','pair'}, dimensions={2}, use_global_device_ids=true | all-gather | bytes 163840 | tf_op jit(solution)/shard_map/all_gather | solution.py:62
  30.6 0.0 copy-done
  30.6 0.4 %fusion.7 = f32[16,4,128]{2,0,1:T(8,128)S(1)} fusion(f32[16,4,512]{2,0,1:T(8,128)S(1)} %all_gather.3, f32[128,512]{1,0:T(8,128)S(1)} %copy-done), kind=kOutput, calls=%fused_computation.20 | convolution fusion | flops 50331648 | bytes 425984 | tf_op jit(solution)/shard_map/kjr,zr->kjz/dot_general | solution.py:60
  31.0 0.6 %copy.71 = f32[16,4,128]{2,1,0:T(4,128)} copy(f32[16,4,128]{2,0,1:T(8,128)S(1)} %fusion.7) | data formatting | bytes 65536
  (5 shorter events, 0.0 us)
Async XLA Ops:
  0.6 30.0 %copy-start = (f32[128,512]{1,0:T(8,128)S(1)}, f32[128,512]{1,0:T(8,128)}, u32[]{:S(2)}) copy-start(f32[128,512]{1,0:T(8,128)} %param.17) | copy-start | bytes 786436
  0.6 4.2 %copy-start.1 = (bf16[1,24,32,128]{3,2,1,0:T(8,128)(2,1)S(1)}, bf16[1,24,32,128]{3,2,1,0:T(8,128)(2,1)}, u32[]{:S(2)}) copy-start(bf16[1,24,32,128]{3,2,1,0:T(8,128)(2,1)} %param.9) | copy-start | bytes 589828
  0.7 4.2 %copy-start.4 = (bf16[4,24,24]{2,1,0:T(8,128)(2,1)S(1)}, bf16[4,24,24]{2,1,0:T(8,128)(2,1)}, u32[]{:S(2)}) copy-start(bf16[4,24,24]{2,1,0:T(8,128)(2,1)} %param.10) | copy-start | bytes 13828
  1.7 10.0 %collective-permute-start = (bf16[1,24,32,128]{3,1,2,0:T(8,128)(2,1)S(1)}, bf16[1,24,32,128]{3,1,2,0:T(8,128)(2,1)S(1)}, u32[]{:S(2)}, u32[]{:S(2)}) collective-permute-start(bf16[1,24,32,128]{3,1,2,0:T(8,128)(2,1)S(1)} %copy.58), channel_id=1, source_target_pairs={{12,0},{0,4},{4,8},{8,12},{13,1},{1,5},{5,9},{9,13},{14,2},{2,6},{... | collective-permute-start | bytes 589832 | tf_op jit(solution)/shard_map/ppermute | solution.py:10
  5.1 0.7 %copy-start.7 = (s32[1,16]{1,0:T(1,128)S(1)}, s32[1,16]{1,0:T(1,128)}, u32[]{:S(2)}) copy-start(s32[1,16]{1,0:T(1,128)} %param.15) | copy-start | bytes 196
  12.0 0.7 %copy-start.6 = (f32[24]{0:T(128)S(1)}, f32[24]{0:T(128)}, u32[]{:S(2)}) copy-start(f32[24]{0:T(128)} %param.11) | copy-start | bytes 292
  12.7 0.7 %copy-start.5 = (bf16[4,24,24]{2,1,0:T(8,128)(2,1)S(1)}, bf16[4,24,24]{2,1,0:T(8,128)(2,1)}, u32[]{:S(2)}) copy-start(bf16[4,24,24]{2,1,0:T(8,128)(2,1)} %param.12) | copy-start | bytes 13828
  13.9 0.7 %copy-start.8 = (f32[24]{0:T(128)S(1)}, f32[24]{0:T(128)}, u32[]{:S(2)}) copy-start(f32[24]{0:T(128)} %param.14) | copy-start | bytes 292
  13.9 0.7 %copy-start.9 = (f32[24]{0:T(128)S(1)}, f32[24]{0:T(128)}, u32[]{:S(2)}) copy-start(f32[24]{0:T(128)} %param.13) | copy-start | bytes 292
  15.5 8.8 %all-to-all-start = ((f32[2,16,128]{2,0,1:T(2,128)}), f32[2,16,128]{2,0,1:T(2,128)S(1)}, u32[]{:S(2)}, u32[]{:S(2)}) async-start(f32[2,16,128]{2,0,1:T(2,128)} %copy.66), calls=%async_computation | async-start | bytes 32768 | tf_op jit(solution)/shard_map/all_to_all | solution.py:58
  24.4 0.6 %copy-start.2 = (f32[4,2,4,128]{3,2,1,0:T(4,128)}, f32[4,2,4,128]{3,2,1,0:T(4,128)S(1)}, u32[]{:S(2)}) copy-start(f32[4,2,4,128]{3,2,1,0:T(4,128)S(1)} %copy.68) | copy-start | bytes 49156
  24.4 0.8 %copy-start.3 = (f32[16,4,128]{2,1,0:T(4,128)S(1)}, f32[16,4,128]{2,1,0:T(4,128)}, u32[]{:S(2)}) copy-start(f32[16,4,128]{2,1,0:T(4,128)} %param.16) | copy-start | bytes 98308
where the time goes:
time: 32 us; the launch traced here: 31.7 us
  waiting for transfers between devices  11.6 us (36%)
  starting transfers between devices  6.36 us (20%)
  blocking collectives  5.4 us (17%)
  local copies, waits for them, and re-layouts  4.83 us (15%)
  matrix products  2.41 us (8%)
  between operations  0.8 us (2%)
    ppermute x1, waiting for transfers between devices, from_behind(): return lax.ppermute(block, axis, route)  6.01 us
    all_to_all x1, waiting for transfers between devices, local(): lax.all_to_all(own_views, 'wide', split_axis=1, concat_axis=0, tiled=True)  5.57 us
    all_gather x1, blocking collectives, local(): lax.all_gather(residual_slab, ('narrow', 'pair'), axis=2, tiled=True)  5.4 us
    unnamed x22, local copies, waits for them, and re-layouts  3.62 us
    all_to_all x1, starting transfers between devices, local(): lax.all_to_all(own_views, 'wide', split_axis=1, concat_axis=0, tiled=True)  3.25 us
    ppermute x1, starting transfers between devices, from_behind(): return lax.ppermute(block, axis, route)  3.1 us
    dot_general x8, matrix products, channel_mix(): jnp.einsum('vcwr,cd->vdwr', inputs, weight, preferred_element_type=jnp.fl...  2.02 us
  transfers between devices with their start and end apart: 2, of which 2 were waited for; matrix products, arithmetic and copies ran while one was open for 2% of the time, Pallas kernels for 0%

commit v1 on v0

v1 whole, which is shorter than its diff:
```python
import functools

import jax
import jax.numpy as jnp
from jax import lax
from jax.experimental import pallas as pl
from jax.experimental.pallas import tpu as pltpu
from jax.sharding import PartitionSpec as P

F32 = jnp.float32
BF16 = jnp.bfloat16


def indices(rows, cols, axis):
    return lax.broadcasted_iota(jnp.int32, (rows, cols), axis).astype(F32)


def div(values, divisor):
    return jnp.floor((values + 0.5) * (1.0 / divisor))


def one_hot(hit):
    return jnp.where(hit, 1.0, 0.0).astype(F32)


def leaky(values):
    return jnp.maximum(values, 0.1 * values)


def nt_dot(left, right, precision=None):
    return lax.dot_general(
        left, right, (((1,), (1,)), ((), ())), precision=precision, preferred_element_type=F32
    )


def angle_matrix(weight, chans):
    size = 4 * chans
    row, col = indices(size, size, 0), indices(size, size, 1)
    row_block, col_block = div(row, chans), div(col, chans)
    spread_row = indices(size, chans, 0)
    left = one_hot(spread_row - chans * div(spread_row, chans) == indices(size, chans, 1)).astype(BF16)
    spread_col = indices(chans, size, 1)
    right = one_hot(spread_col - chans * div(spread_col, chans) == indices(chans, size, 0)).astype(BF16)
    parity, side = div(row_block, 2), div(col_block, 2)
    same = (row_block - 2 * parity) == (col_block - 2 * side)
    total = jnp.zeros((size, size), F32)
    for tap in range(4):
        spread = nt_dot(left, weight[tap]).astype(BF16)
        spread = jnp.dot(spread, right, preferred_element_type=F32)
        total = jnp.where(same & (parity + 2 * side == tap), spread, total)
    return total.astype(BF16)


def column_matrix(weight, chans, outs, first, last):
    rows, cols = chans * outs, 2 * (outs + 1) * chans
    row, col = indices(rows, cols, 0), indices(rows, cols, 1)
    out_col = row - outs * div(row, outs)
    in_col = div(col, chans)
    left = one_hot(div(indices(rows, chans, 0), outs) == indices(rows, chans, 1)).astype(BF16)
    spread_col = indices(chans, cols, 1)
    right = one_hot(spread_col - chans * div(spread_col, chans) == indices(chans, cols, 0)).astype(BF16)
    total = jnp.zeros((rows, cols), F32)
    for tap in range(4):
        spread = nt_dot(left, weight[tap]).astype(BF16)
        spread = jnp.dot(spread, right, preferred_element_type=F32)
        total = jnp.where(in_col - 2 * out_col == tap, spread, total)
    outside = ((in_col == 0) & first) | ((in_col == 2 * outs + 1) & last)
    return jnp.where(outside, 0.0, total).astype(BF16)


def kernel(
    wide, narrow, pair, outs,
    x_hbm, aw_hbm, ab_hbm, cw_hbm, cb_hbm, hw_hbm, sv_hbm, meas_hbm, rw_hbm,
    pred_hbm, adj_hbm,
    x_in, x_cols, x_all, aw, ab, cw, cb, hw, sv_all, sv_s, meas_all, rows_m, rw,
    pred_all, pred_out, adj_out, picks,
    in_sem, sv_sem, out_sem, x_send, x_recv, m_send, m_recv, s_send, s_recv, p_send, p_recv,
):
    me = lax.axis_index("wide")
    my_n, my_p = lax.axis_index("narrow"), lax.axis_index("pair")
    group = narrow * pair
    my_g = my_n * pair + my_p
    chans, lanes = x_in.shape[1], x_in.shape[3]
    views = x_in.shape[0]
    pairs = outs + 1
    all_views = wide * views
    keep = meas_all.shape[1]

    def row_peer(step):
        other = lax.rem(my_g + step, group)
        return other, {"narrow": lax.div(other, pair), "pair": lax.rem(other, pair)}

    barrier = pltpu.get_barrier_semaphore()
    for step in range(1, wide):
        pl.semaphore_signal(
            barrier, inc=1, device_id={"wide": lax.rem(me + step, wide)}, device_id_type=pl.DeviceIdType.MESH
        )
    for step in range(1, group):
        pl.semaphore_signal(
            barrier, inc=1, device_id=row_peer(step)[1], device_id_type=pl.DeviceIdType.MESH
        )

    loads = [
        pltpu.make_async_copy(source, target, in_sem.at[spot])
        for spot, (source, target) in enumerate(
            [
                (x_hbm, x_in), (aw_hbm, aw), (ab_hbm, ab), (cw_hbm, cw), (cb_hbm, cb), (hw_hbm, hw),
                (rw_hbm, rw), (meas_hbm, meas_all.at[my_g]), (sv_hbm, sv_all.at[my_n]),
            ]
        )
    ]
    for load in loads:
        load.start()

    loads[0].wait()
    blank = jnp.zeros((1, chans, lanes), F32)
    for view in range(views):
        turned = jnp.swapaxes(x_in[view].astype(F32), 0, 1)
        padded = jnp.concatenate([blank, turned, blank], axis=0)
        x_cols[view] = padded.reshape(x_cols.shape[1], 2 * chans, lanes).astype(BF16)

    pl.semaphore_wait(barrier, wide - 1 + group - 1)

    order = sorted(range(1, wide), key=lambda step: abs(step - wide // 2))
    sends = []
    for step in order:
        target = lax.rem(me + step, wide)
        sends.append(
            pltpu.make_async_remote_copy(
                src_ref=x_cols.at[:, pl.ds(outs * target, pairs)],
                dst_ref=x_all.at[me],
                send_sem=x_send.at[step],
                recv_sem=x_recv.at[me],
                device_id={"wide": target},
                device_id_type=pl.DeviceIdType.MESH,
            )
        )
        sends[-1].start()
    loads[7].wait()
    loads[8].wait()
    for step in range(1, group):
        other, where = row_peer(step)
        sends.append(
            pltpu.make_async_remote_copy(
                src_ref=meas_all.at[my_g],
                dst_ref=meas_all.at[my_g],
                send_sem=m_send.at[step],
                recv_sem=m_recv.at[my_g],
                device_id=where,
                device_id_type=pl.DeviceIdType.MESH,
            )
        )
        sends[-1].start()
    for step in range(1, narrow):
        sends.append(
            pltpu.make_async_remote_copy(
                src_ref=sv_all.at[my_n],
                dst_ref=sv_all.at[my_n],
                send_sem=s_send.at[step],
                recv_sem=s_recv.at[my_n],
                device_id={"narrow": lax.rem(my_n + step, narrow)},
                device_id_type=pl.DeviceIdType.MESH,
            )
        )
        sends[-1].start()
    x_all[me] = x_cols[:, pl.ds(outs * me, pairs)]

    for load in loads[1:7]:
        load.wait()
    angle = angle_matrix(aw, chans)
    column = column_matrix(cw, chans, outs, me == 0, me == wide - 1)
    pick_row = indices(4 * chans, chans, 0)
    angle_bias = jnp.sum(
        one_hot(pick_row - chans * div(pick_row, chans) == indices(4 * chans, chans, 1)) * ab[...],
        axis=1, keepdims=True,
    )
    head_hot = one_hot(div(indices(outs * chans, chans, 0), outs) == indices(outs * chans, chans, 1))
    column_bias = jnp.sum(head_hot * cb[...], axis=1, keepdims=True)
    head = jnp.sum(head_hot * hw[...], axis=1, keepdims=True)

    def wait_for(block, sem):
        pltpu.make_async_remote_copy(
            src_ref=block, dst_ref=block, send_sem=x_send.at[0], recv_sem=sem,
            device_id={"wide": me}, device_id_type=pl.DeviceIdType.MESH,
        ).wait_recv()

    for step in range(1, group):
        other = row_peer(step)[0]
        wait_for(meas_all.at[other], m_recv.at[other])
    for step in range(1, narrow):
        other = lax.rem(my_n + step, narrow)
        wait_for(sv_all.at[other], s_recv.at[other])
    fetch = pltpu.make_async_copy(sv_all, sv_s, sv_sem)
    fetch.start()
    for block in range(group):
        for spot in range(keep):
            rows_m[pl.ds(spot * outs, outs), pl.ds(block * lanes, lanes)] = meas_all[block, spot]
    measured = nt_dot(rows_m[...], rw[...], lax.Precision.HIGHEST)
    rows_m[:, : rw.shape[0]] = measured
    fetch.wait()

    fold = 8 // outs
    arrived = set()
    for step in range(wide):
        for near in (step, step + wide - 1):
            near %= wide
            if near and near not in arrived:
                source = lax.rem(me + near, wide)
                wait_for(x_all.at[source], x_recv.at[source])
                arrived.add(near)
        for view in range(views):
            now = lax.rem(me + step, wide) * views + view
            before = lax.rem(now + all_views - 1, all_views)
            current = x_all[lax.div(now, views), lax.rem(now, views)]
            previous = x_all[lax.div(before, views), lax.rem(before, views)]
            inputs = jnp.concatenate(
                [
                    jnp.concatenate([current[spot], previous[spot]], axis=0)
                    for spot in range(pairs)
                ],
                axis=1,
            )
            raised = jnp.dot(angle, inputs, preferred_element_type=F32)
            raised = leaky(raised + angle_bias).astype(BF16)
            stacked = jnp.concatenate(
                [
                    jnp.concatenate(
                        [
                            raised[parity * 2 * chans : (parity + 1) * 2 * chans, spot * lanes : (spot + 1) * lanes]
                            for spot in range(pairs)
                        ],
                        axis=0,
                    )
                    for parity in range(2)
                ],
                axis=1,
            )
            hidden = jnp.dot(column, stacked, preferred_element_type=F32)
            hidden = leaky(hidden + column_bias) * head
            summed = jnp.sum(hidden.reshape(chans // fold, 8, 2 * lanes), axis=0)
            even, odd = summed[:, :lanes], summed[:, lanes:]
            shift = outs
            while shift < 8:
                even = even + pltpu.roll(even, shift, axis=0)
                odd = odd + pltpu.roll(odd, shift, axis=0)
                shift *= 2
            row = lax.broadcasted_iota(jnp.int32, even.shape, 0)
            both = jnp.where(row < outs, even, odd)
            pred_all[my_g, now] = both
            pred_out[2 * now] = both[:outs]
            pred_out[2 * now + 1] = both[outs : 2 * outs]

    finals = []
    for step in range(1, group):
        other, where = row_peer(step)
        finals.append(
            pltpu.make_async_remote_copy(
                src_ref=pred_all.at[my_g],
                dst_ref=pred_all.at[my_g],
                send_sem=p_send.at[step],
                recv_sem=p_recv.at[my_g],
                device_id=where,
                device_id_type=pl.DeviceIdType.MESH,
            )
        )
        finals[-1].start()
    store = pltpu.make_async_copy(pred_out, pred_hbm, out_sem.at[0])
    store.start()
    for step in range(1, group):
        other = row_peer(step)[0]
        wait_for(pred_all.at[other], p_recv.at[other])

    for band in range(narrow):
        total = jnp.zeros((8 * all_views, rw.shape[0]), F32)
        for block in range(band * pair, (band + 1) * pair):
            total += nt_dot(
                pred_all[block].reshape(8 * all_views, lanes),
                rw[:, block * lanes : (block + 1) * lanes],
                lax.Precision.HIGHEST,
            )
        for view in range(all_views):
            picks[band, 2 * view] = total[8 * view : 8 * view + outs]
            picks[band, 2 * view + 1] = total[8 * view + outs : 8 * view + 2 * outs]
    for spot in range(keep):
        value = picks[0, sv_s[0, 0, spot]]
        for band in range(1, narrow):
            value = value + picks[band, sv_s[band, 0, spot]]
        adj_out[spot] = value - rows_m[pl.ds(spot * outs, outs), : rw.shape[0]]
    last = pltpu.make_async_copy(adj_out, adj_hbm, out_sem.at[1])
    last.start()
    for send in sends + finals:
        send.wait_send()
    store.wait()
    last.wait()


def local(
    wide, narrow, pair,
    low_sino, angle_weight, angle_bias, column_weight, column_bias, head_weight,
    sparse_views, measured, row_weights,
):
    views, chans, cols, lanes = low_sino.shape
    keep, outs, _ = measured.shape
    depth = row_weights.shape[0]
    group = narrow * pair
    all_views = wide * views
    any_space = pl.BlockSpec(memory_space=pl.ANY)
    dma = pltpu.SemaphoreType.DMA
    return pl.pallas_call(
        functools.partial(kernel, wide, narrow, pair, outs),
        out_shape=(
            jax.ShapeDtypeStruct((2 * all_views, outs, lanes), F32),
            jax.ShapeDtypeStruct((keep, outs, depth), F32),
        ),
        in_specs=[any_space] * 9,
        out_specs=(any_space, any_space),
        scratch_shapes=[
            pltpu.VMEM(low_sino.shape, BF16),
            pltpu.VMEM((views, cols // 2 + 1, 2 * chans, lanes), BF16),
            pltpu.VMEM((wide, views, outs + 1, 2 * chans, lanes), BF16),
            pltpu.VMEM(angle_weight.shape, BF16),
            pltpu.VMEM((1, chans), F32),
            pltpu.VMEM(column_weight.shape, BF16),
            pltpu.VMEM((1, chans), F32),
            pltpu.VMEM((1, chans), F32),
            pltpu.VMEM((narrow, 1, keep), jnp.int32),
            pltpu.SMEM((narrow, 1, keep), jnp.int32),
            pltpu.VMEM((group, keep, outs, lanes), F32),
            pltpu.VMEM((keep * outs, group * lanes), F32),
            pltpu.VMEM(row_weights.shape, F32),
            pltpu.VMEM((group, all_views, 8, lanes), F32),
            pltpu.VMEM((2 * all_views, outs, lanes), F32),
            pltpu.VMEM((keep, outs, depth), F32),
            pltpu.VMEM((narrow, 2 * all_views, outs, depth), F32),
            dma((9,)), dma, dma((2,)),
            dma((wide,)), dma((wide,)),
            dma((group,)), dma((group,)),
            dma((narrow,)), dma((narrow,)),
            dma((group,)), dma((group,)),
        ],
        compiler_params=pltpu.CompilerParams(collective_id=0, has_side_effects=True),
    )(
        low_sino, angle_weight, angle_bias[None], column_weight, column_bias[None], head_weight[None],
        sparse_views, measured, row_weights,
    )


def solution(mesh):
    in_specs = (
        P(("parts", "wide"), None, None, ("narrow", "pair")),
        P(),
        P(),
        P(),
        P(),
        P(),
        P(("parts", "narrow"), None),
        P("parts", "wide", ("narrow", "pair")),
        P(("narrow", "pair"), None),
    )
    out_specs = (P("parts", "wide", ("narrow", "pair")), P("parts", "wide", ("narrow", "pair")))
    body = functools.partial(local, mesh.shape["wide"], mesh.shape["narrow"], mesh.shape["pair"])
    return jax.shard_map(body, mesh=mesh, in_specs=in_specs, out_specs=out_specs, check_vma=False)
```

time: 32 us -> 19 us (0.59)
  Pallas kernels: 0 us -> 16.2 us
  waiting for transfers between devices: 11.6 us -> 0 us
  starting transfers between devices: 6.36 us -> 0 us
  blocking collectives: 5.4 us -> 0 us
  local copies, waits for them, and re-layouts: 4.83 us -> 1.95 us
  matrix products: 2.41 us -> 0 us
    pallas_call x0 -> x1, Pallas kernels: none -> 16.2 us  [local(): pl.pallas_call(functools.partial(kernel, wide, narrow, pair, outs), out_s...]
    ppermute x1 -> x0, waiting for transfers between devices: 6.01 us -> none  [from_behind(): return lax.ppermute(block, axis, route)]
    all_to_all x1 -> x0, waiting for transfers between devices: 5.57 us -> none  [local(): lax.all_to_all(own_views, 'wide', split_axis=1, concat_axis=0, tiled=True)]
    all_gather x1 -> x0, blocking collectives: 5.4 us -> none  [local(): lax.all_gather(residual_slab, ('narrow', 'pair'), axis=2, tiled=True)]
    all_to_all x1 -> x0, starting transfers between devices: 3.25 us -> none  [local(): lax.all_to_all(own_views, 'wide', split_axis=1, concat_axis=0, tiled=True)]
    ppermute x1 -> x0, starting transfers between devices: 3.1 us -> none  [from_behind(): return lax.ppermute(block, axis, route)]
    dot_general x9 -> x0, matrix products: 2.41 us -> none  [the longest x8 2.02 us: channel_mix(): jnp.einsum('vcwr,cd->vdwr', inputs, weight, preferred_element_type=jnp.fl...]
    unnamed x22 -> x4, local copies, waits for them, and re-layouts: 3.62 us -> 1.95 us
  transfers between devices with their start and end apart: 2 -> 0, of which waited for: 2 -> 0; matrix products, arithmetic and copies ran while one was open for 2% -> 0% of each run, Pallas kernels for 0% -> 0%
where the time goes in v1:
time: 19 us; the launch traced here: 18.8 us
  Pallas kernels  16.2 us (85%)
  local copies, waits for them, and re-layouts  1.95 us (10%)
  between operations  0.65 us (3%)
    pallas_call x1, Pallas kernels, local(): pl.pallas_call(functools.partial(kernel, wide, narrow, pair, outs), out_s...  16.2 us
    unnamed x4, local copies, waits for them, and re-layouts  1.95 us

profile of v1, /device:TPU:0, one launch (start us, length us, event | category | flops | bytes accessed | tf_op | source)
XLA Modules:
  0.0 18.8 jit_solution(18205502891695514420)
XLA Ops:
  0.6 16.2 %shard_map.104 = (f32[8,4,128]{2,1,0:T(4,128)}, f32[16,4,128]{2,1,0:T(4,128)}) custom-call(bf16[1,24,32,128]{3,2,1,0:T(8,128)(2,1)} %x_hbm.1, bf16[4,24,24]{2,1,0:T(8,128)(2,1)} %aw_hbm.1, f32[1,24]{1,0:T(1,128)} %bitcast.3, bf16[4,24,24]{2,1,0:T(8,128)(2,1)} %cw_hbm.1, f32[1,24]{1,0:T(1,128)} %bitcast.4, f32[1,24]{1,0:T(1,128)} %bitcast.5, s32[1,16]{1,0:T(1,128)} %sv_hbm.1, ...), custom_call_target="tpu_custom_call" | custom-call | tf_op jit(solution)/shard_map/pallas_call | solution.py:309
  16.8 0.0 copy-start
  16.8 1.3 %copy.13 = f32[8,4,128]{2,1,0:T(4,128)} copy(f32[8,4,128]{2,1,0:T(4,128)} %get-tuple-element.4) | data formatting | bytes 32768
  18.2 0.0 copy-done
  18.2 0.6 %copy.14 = f32[16,4,128]{2,1,0:T(4,128)} copy(f32[16,4,128]{2,1,0:T(4,128)S(1)} %copy-done) | data formatting | bytes 65536
Async XLA Ops:
  16.8 1.3 %copy-start = (f32[16,4,128]{2,1,0:T(4,128)S(1)}, f32[16,4,128]{2,1,0:T(4,128)}, u32[]{:S(2)}) copy-start(f32[16,4,128]{2,1,0:T(4,128)} %get-tuple-element.5) | copy-start | bytes 98308

commit v2 on v1

--- a/solution.py
+++ b/solution.py
@@ -71,10 +71,10 @@
 def kernel(
     wide, narrow, pair, outs,
     x_hbm, aw_hbm, ab_hbm, cw_hbm, cb_hbm, hw_hbm, sv_hbm, meas_hbm, rw_hbm,
-    pred_hbm, adj_hbm,
+    pred_out, adj_out,
     x_in, x_cols, x_all, aw, ab, cw, cb, hw, sv_all, sv_s, meas_all, rows_m, rw,
-    pred_all, pred_out, adj_out, picks,
-    in_sem, sv_sem, out_sem, x_send, x_recv, m_send, m_recv, s_send, s_recv, p_send, p_recv,
+    pred_all, picks,
+    in_sem, sv_sem, x_send, x_recv, m_send, m_recv, s_send, s_recv, p_send, p_recv,
 ):
     me = lax.axis_index("wide")
     my_n, my_p = lax.axis_index("narrow"), lax.axis_index("pair")
@@ -264,8 +264,6 @@
             )
         )
         finals[-1].start()
-    store = pltpu.make_async_copy(pred_out, pred_hbm, out_sem.at[0])
-    store.start()
     for step in range(1, group):
         other = row_peer(step)[0]
         wait_for(pred_all.at[other], p_recv.at[other])
@@ -286,12 +284,19 @@
         for band in range(1, narrow):
             value = value + picks[band, sv_s[band, 0, spot]]
         adj_out[spot] = value - rows_m[pl.ds(spot * outs, outs), : rw.shape[0]]
-    last = pltpu.make_async_copy(adj_out, adj_hbm, out_sem.at[1])
-    last.start()
     for send in sends + finals:
         send.wait_send()
-    store.wait()
-    last.wait()
+
+
+def write_out(pred_in, adj_in, pred_hbm, adj_hbm, sems):
+    copies = [
+        pltpu.make_async_copy(pred_in, pred_hbm, sems.at[0]),
+        pltpu.make_async_copy(adj_in, adj_hbm, sems.at[1]),
+    ]
+    for copy in copies:
+        copy.start()
+    for copy in copies:
+        copy.wait()
 
 
 def local(
@@ -306,14 +311,13 @@
     all_views = wide * views
     any_space = pl.BlockSpec(memory_space=pl.ANY)
     dma = pltpu.SemaphoreType.DMA
-    return pl.pallas_call(
+    vmem = pl.BlockSpec(memory_space=pltpu.VMEM)
+    shapes = ((2 * all_views, outs, lanes), (keep, outs, depth))
+    held = pl.pallas_call(
         functools.partial(kernel, wide, narrow, pair, outs),
-        out_shape=(
-            jax.ShapeDtypeStruct((2 * all_views, outs, lanes), F32),
-            jax.ShapeDtypeStruct((keep, outs, depth), F32),
-        ),
+        out_shape=tuple(pltpu.VMEM(shape, F32) for shape in shapes),
         in_specs=[any_space] * 9,
-        out_specs=(any_space, any_space),
+        out_specs=(vmem, vmem),
         scratch_shapes=[
             pltpu.VMEM(low_sino.shape, BF16),
             pltpu.VMEM((views, cols // 2 + 1, 2 * chans, lanes), BF16),
@@ -329,10 +333,8 @@
             pltpu.VMEM((keep * outs, group * lanes), F32),
             pltpu.VMEM(row_weights.shape, F32),
             pltpu.VMEM((group, all_views, 8, lanes), F32),
-            pltpu.VMEM((2 * all_views, outs, lanes), F32),
-            pltpu.VMEM((keep, outs, depth), F32),
             pltpu.VMEM((narrow, 2 * all_views, outs, depth), F32),
-            dma((9,)), dma, dma((2,)),
+            dma((9,)), dma,
             dma((wide,)), dma((wide,)),
             dma((group,)), dma((group,)),
             dma((narrow,)), dma((narrow,)),
@@ -343,6 +345,13 @@
         low_sino, angle_weight, angle_bias[None], column_weight, column_bias[None], head_weight[None],
         sparse_views, measured, row_weights,
     )
+    return pl.pallas_call(
+        write_out,
+        out_shape=tuple(jax.ShapeDtypeStruct(shape, F32) for shape in shapes),
+        in_specs=[vmem, vmem],
+        out_specs=(any_space, any_space),
+        scratch_shapes=[dma((2,))],
+    )(*(pltpu.with_memory_space_constraint(x, pltpu.VMEM) for x in held))
 
 
 def solution(mesh):

time: 19 us -> 17 us (0.89)
  local copies, waits for them, and re-layouts: 1.95 us -> 0 us
    unnamed x4 -> x0, local copies, waits for them, and re-layouts: 1.95 us -> none
    pallas_call x0 -> x1, Pallas kernels: none -> 0.64 us  [local(): pl.pallas_call(write_out, out_shape=tuple((jax.ShapeDtypeStruct(shape, F3...]
    pallas_call x1, Pallas kernels: 16.2 us -> 15.6 us  [local(): pl.pallas_call(functools.partial(kernel, wide, narrow, pair, outs), out_s...]
where the time goes in v2:
time: 17 us; the launch traced here: 16.9 us
  Pallas kernels  16.2 us (95%)
  between operations  0.64 us (4%)
    pallas_call x1, Pallas kernels, local(): pl.pallas_call(functools.partial(kernel, wide, narrow, pair, outs), out_s...  15.6 us
    pallas_call x1, Pallas kernels, local(): pl.pallas_call(write_out, out_shape=tuple((jax.ShapeDtypeStruct(shape, F3...  0.64 us

profile of v2, /device:TPU:0, one launch (start us, length us, event | category | flops | bytes accessed | tf_op | source)
XLA Modules:
  0.0 16.9 jit_solution(5109383944576153035)
XLA Ops:
  0.6 15.6 %shard_map.104 = (f32[8,4,128]{2,1,0:T(4,128)S(1)}, f32[16,4,128]{2,1,0:T(4,128)S(1)}) custom-call(bf16[1,24,32,128]{3,2,1,0:T(8,128)(2,1)} %x_hbm.1, bf16[4,24,24]{2,1,0:T(8,128)(2,1)} %aw_hbm.1, f32[1,24]{1,0:T(1,128)} %bitcast.3, bf16[4,24,24]{2,1,0:T(8,128)(2,1)} %cw_hbm.1, f32[1,24]{1,0:T(1,128)} %bitcast.4, f32[1,24]{1,0:T(1,128)} %bitcast.5, ...), custom_call_target="tpu_custom_call" | custom-call | tf_op jit(solution)/shard_map/pallas_call | solution.py:316
  16.2 0.6 %shard_map.105 = (f32[8,4,128]{2,1,0:T(4,128)}, f32[16,4,128]{2,1,0:T(4,128)}) custom-call(f32[8,4,128]{2,1,0:T(4,128)S(1)} %get-tuple-element.4.pred_in, f32[16,4,128]{2,1,0:T(4,128)S(1)} %get-tuple-element.5.adj_in), custom_call_target="tpu_custom_call" | custom-call | tf_op jit(solution)/shard_map/pallas_call | solution.py:348

commit v3 on v2

--- a/solution.py
+++ b/solution.py
@@ -121,7 +121,7 @@
 
     pl.semaphore_wait(barrier, wide - 1 + group - 1)
 
-    order = sorted(range(1, wide), key=lambda step: abs(step - wide // 2))
+    order = range(1, wide)
     sends = []
     for step in order:
         target = lax.rem(me + step, wide)
@@ -136,8 +136,20 @@
             )
         )
         sends[-1].start()
+    loads[8].wait()
+    for step in range(1, narrow):
+        sends.append(
+            pltpu.make_async_remote_copy(
+                src_ref=sv_all.at[my_n],
+                dst_ref=sv_all.at[my_n],
+                send_sem=s_send.at[step],
+                recv_sem=s_recv.at[my_n],
+                device_id={"narrow": lax.rem(my_n + step, narrow)},
+                device_id_type=pl.DeviceIdType.MESH,
+            )
+        )
+        sends[-1].start()
     loads[7].wait()
-    loads[8].wait()
     for step in range(1, group):
         other, where = row_peer(step)
         sends.append(
@@ -147,18 +159,6 @@
                 send_sem=m_send.at[step],
                 recv_sem=m_recv.at[my_g],
                 device_id=where,
-                device_id_type=pl.DeviceIdType.MESH,
-            )
-        )
-        sends[-1].start()
-    for step in range(1, narrow):
-        sends.append(
-            pltpu.make_async_remote_copy(
-                src_ref=sv_all.at[my_n],
-                dst_ref=sv_all.at[my_n],
-                send_sem=s_send.at[step],
-                recv_sem=s_recv.at[my_n],
-                device_id={"narrow": lax.rem(my_n + step, narrow)},
                 device_id_type=pl.DeviceIdType.MESH,
             )
         )
@@ -183,21 +183,6 @@
             src_ref=block, dst_ref=block, send_sem=x_send.at[0], recv_sem=sem,
             device_id={"wide": me}, device_id_type=pl.DeviceIdType.MESH,
         ).wait_recv()
-
-    for step in range(1, group):
-        other = row_peer(step)[0]
-        wait_for(meas_all.at[other], m_recv.at[other])
-    for step in range(1, narrow):
-        other = lax.rem(my_n + step, narrow)
-        wait_for(sv_all.at[other], s_recv.at[other])
-    fetch = pltpu.make_async_copy(sv_all, sv_s, sv_sem)
-    fetch.start()
-    for block in range(group):
-        for spot in range(keep):
-            rows_m[pl.ds(spot * outs, outs), pl.ds(block * lanes, lanes)] = meas_all[block, spot]
-    measured = nt_dot(rows_m[...], rw[...], lax.Precision.HIGHEST)
-    rows_m[:, : rw.shape[0]] = measured
-    fetch.wait()
 
     fold = 8 // outs
     arrived = set()
@@ -266,6 +251,21 @@
         finals[-1].start()
     for step in range(1, group):
         other = row_peer(step)[0]
+        wait_for(meas_all.at[other], m_recv.at[other])
+    for step in range(1, narrow):
+        other = lax.rem(my_n + step, narrow)
+        wait_for(sv_all.at[other], s_recv.at[other])
+    fetch = pltpu.make_async_copy(sv_all, sv_s, sv_sem)
+    fetch.start()
+    for block in range(group):
+        for spot in range(keep):
+            rows_m[pl.ds(spot * outs, outs), pl.ds(block * lanes, lanes)] = meas_all[block, spot]
+    measured = nt_dot(rows_m[...], rw[...], lax.Precision.HIGH)
+    rows_m[:, : rw.shape[0]] = measured
+    fetch.wait()
+
+    for step in range(1, group):
+        other = row_peer(step)[0]
         wait_for(pred_all.at[other], p_recv.at[other])
 
     for band in range(narrow):
@@ -274,7 +274,7 @@
             total += nt_dot(
                 pred_all[block].reshape(8 * all_views, lanes),
                 rw[:, block * lanes : (block + 1) * lanes],
-                lax.Precision.HIGHEST,
+                lax.Precision.HIGH,
             )
         for view in range(all_views):
             picks[band, 2 * view] = total[8 * view : 8 * view + outs]

time: 17 us -> 16.6 us (0.976)
  Pallas kernels: 16.2 us -> 15.8 us
    pallas_call x1, Pallas kernels: 15.6 us -> 15.1 us  [local(): pl.pallas_call(functools.partial(kernel, wide, narrow, pair, outs), out_s...]
where the time goes in v3:
time: 16.6 us; the launch traced here: 16.4 us
  Pallas kernels  15.8 us (95%)
  between operations  0.64 us (4%)
    pallas_call x1, Pallas kernels, local(): pl.pallas_call(functools.partial(kernel, wide, narrow, pair, outs), out_s...  15.1 us
    pallas_call x1, Pallas kernels, local(): pl.pallas_call(write_out, out_shape=tuple((jax.ShapeDtypeStruct(shape, F3...  0.64 us

profile of v3, /device:TPU:0, one launch (start us, length us, event | category | flops | bytes accessed | tf_op | source)
XLA Modules:
  0.0 16.4 jit_solution(11391038034454586921)
XLA Ops:
  0.6 15.1 %shard_map.104 = (f32[8,4,128]{2,1,0:T(4,128)S(1)}, f32[16,4,128]{2,1,0:T(4,128)S(1)}) custom-call(bf16[1,24,32,128]{3,2,1,0:T(8,128)(2,1)} %x_hbm.1, bf16[4,24,24]{2,1,0:T(8,128)(2,1)} %aw_hbm.1, f32[1,24]{1,0:T(1,128)} %bitcast.3, bf16[4,24,24]{2,1,0:T(8,128)(2,1)} %cw_hbm.1, f32[1,24]{1,0:T(1,128)} %bitcast.4, f32[1,24]{1,0:T(1,128)} %bitcast.5, ...), custom_call_target="tpu_custom_call" | custom-call | tf_op jit(solution)/shard_map/pallas_call | solution.py:316
  15.8 0.6 %shard_map.105 = (f32[8,4,128]{2,1,0:T(4,128)}, f32[16,4,128]{2,1,0:T(4,128)}) custom-call(f32[8,4,128]{2,1,0:T(4,128)S(1)} %get-tuple-element.4.pred_in, f32[16,4,128]{2,1,0:T(4,128)S(1)} %get-tuple-element.5.adj_in), custom_call_target="tpu_custom_call" | custom-call | tf_op jit(solution)/shard_map/pallas_call | solution.py:348
